TPU v7x, 128 devices: a whole 4x4x4 slice. The times are simulated.
128 devices in a mesh: batch: 8 (over y, core), replica: 4 (over x), proto: 4 (over z).
Axes of the slice: x: 4, y: 4, z: 4, core: 2. Of those that a mesh axis runs over, the one named last changes fastest.
Arguments:
- view_one: bfloat16 [16384, 512], P(('batch', 'replica')), may hold values from -4 to 4
- view_two: bfloat16 [16384, 512], P(('batch', 'replica')), may hold values from -4 to 4
- prototypes: bfloat16 [16384, 512], P('proto'), may hold values from -8 to 8
- pairing: int32 [32, 512], P(('batch', 'replica')), may hold values from 0 to 511, as said below
Outputs:
- grad_one: float32 [16384, 512], P(('batch', 'replica'))
- grad_two: float32 [16384, 512], P(('batch', 'replica'))
- grad_prototypes: float32 [16384, 512], P('proto')
Inputs may be any that keep to these rules, and one draw needn't show every extreme that they name: Each row of pairing names every one of 0 to 511 once.
All inputs are finite; a program needn't handle non-finite values.
Results may differ from a plain program's by a relative error of at most 0.0018.
The roundings to bfloat16 on the way count: a program that leaves them out, or rounds other values in their place, can miss the bound.
Values sent between devices are 32-bit elements; how exact they have to be, the bound alone decides.
A program may use at most 128 MiB of HBM per device.

v0:
```python
import jax
import jax.numpy as jnp
from jax import lax
from jax.sharding import PartitionSpec as P

ITERS = 3
sink_eps = 0.05
softness_divisor = 0.1


def unit_rows(x):
    xf = x.astype(jnp.float32)
    inv = lax.rsqrt(jnp.sum(xf * xf, -1, keepdims=True) + 1e-06)
    return (xf * inv, inv)


def unit_back(grad, unit, inv):
    return inv * (grad - unit * jnp.sum(unit * grad, -1, keepdims=True))


def balance_single(similarity_logits):
    codes = jnp.exp(similarity_logits / sink_eps)
    for step in range(ITERS):
        codes = codes / lax.psum(jnp.sum(codes, 0, keepdims=True), ("batch", "replica"))
        codes = codes / lax.psum(jnp.sum(codes, 1, keepdims=True), "proto")
    return codes


def per_device(view_one, view_two, prototypes, pairing):
    unit_one, inv_one = unit_rows(view_one)
    unit_two, inv_two = unit_rows(view_two)
    unit_proto, inv_proto = unit_rows(prototypes)
    low_one = unit_one.astype(jnp.bfloat16)
    low_two = unit_two.astype(jnp.bfloat16)
    low_proto = unit_proto.astype(jnp.bfloat16)
    dims = (((1,), (1,)), ((), ()))
    logits_first_view = lax.dot_general(
        low_one, low_proto, dims, preferred_element_type=jnp.float32
    )
    logits_second_view = lax.dot_general(
        low_two, low_proto, dims, preferred_element_type=jnp.float32
    )
    codes_one = balance_single(logits_first_view)
    codes_two = balance_single(logits_second_view)
    exponent_first_view = jnp.exp(logits_first_view / softness_divisor)
    exponent_second_view = jnp.exp(logits_second_view / softness_divisor)
    total_one, total_two = lax.psum(
        (
            jnp.sum(exponent_first_view, 1, keepdims=True),
            jnp.sum(exponent_second_view, 1, keepdims=True),
        ),
        "proto",
    )
    local_rows = view_one.shape[0]
    partner = pairing[0]
    inverse = (
        jnp.zeros((local_rows,), jnp.int32).at[partner].set(jnp.arange(local_rows, dtype=jnp.int32))
    )
    target_one = codes_two[partner]
    target_two = codes_one[inverse]
    gradient_scale_factor = 0.5 / softness_divisor
    dscore_one = (gradient_scale_factor * (exponent_first_view / total_one - target_one)).astype(
        jnp.bfloat16
    )
    dscore_two = (gradient_scale_factor * (exponent_second_view / total_two - target_two)).astype(
        jnp.bfloat16
    )
    part_one = jnp.dot(dscore_one, low_proto, preferred_element_type=jnp.float32)
    part_two = jnp.dot(dscore_two, low_proto, preferred_element_type=jnp.float32)
    dunit_one, dunit_two = lax.psum((part_one, part_two), "proto")
    grad_one = unit_back(dunit_one, unit_one, inv_one)
    grad_two = unit_back(dunit_two, unit_two, inv_two)
    tdims = (((0,), (0,)), ((), ()))
    local_grad = lax.dot_general(dscore_one, low_one, tdims, preferred_element_type=jnp.float32)
    local_grad = local_grad + lax.dot_general(
        dscore_two, low_two, tdims, preferred_element_type=jnp.float32
    )
    dunit_proto = lax.psum(local_grad, ("batch", "replica"))
    grad_prototypes = unit_back(dunit_proto, unit_proto, inv_proto)
    return (grad_one, grad_two, grad_prototypes)


def solution(mesh):
    placed = (
        P(("batch", "replica"), None),
        P(("batch", "replica"), None),
        P("proto", None),
        P(("batch", "replica"), None),
    )
    return jax.shard_map(
        per_device,
        mesh=mesh,
        in_specs=placed,
        out_specs=(P(("batch", "replica"), None), P(("batch", "replica"), None), P("proto", None)),
        check_vma=False,
    )
```

profile of v0, /device:TPU:1, one launch (start us, length us, event | category | flops | bytes accessed | tf_op | source)
XLA Modules:
  0.0 741.3 jit_solution(12639128571758803586)
XLA Ops:
  7.2 3.1 fusion.18
  12.8 8.5 %fusion.31 = (f32[4096]{0:T(1024)S(1)}, f32[512,4096]{1,0:T(8,128)}) fusion(bf16[4096,512]{1,0:T(8,128)(2,1)} %param.6, f32[4096]{0:T(1024)S(1)} %add_rsqrt_fusion, bf16[512,512]{1,0:T(8,128)(2,1)} %param.5, f32[512]{0:T(512)S(1)} %add_rsqrt_fusion.1), kind=kOutput, calls=%fused_computation.49 | convolution fusion | flops 2158751744 | bytes 13142016 | tf_op jit(solution)/shard_map/dot_general | solution.py:40
  21.3 5.0 fusion.32
  26.2 124.9 %all-reduce.2 = (f32[4096]{0:T(1024)S(1)}, f32[4096]{0:T(1024)S(1)}) all-reduce(f32[4096]{0:T(1024)S(1)} %get-tuple-element.25, f32[4096]{0:T(1024)S(1)} %get-tuple-element.27), channel_id=1, replica_groups=mesh['batch'=8,'replica'=4,'proto'=4] {'batch','replica'}, use_global_device_ids=true, to_apply=%region_6.0 | all-reduce | flops 8192 | bytes 65536 | tf_op jit(solution)/shard_map/psum | solution.py:24
  151.1 8.0 %fusion.30 = (f32[512]{0:T(512)S(1)}, f32[512]{0:T(512)S(1)}, f32[512]{0:T(512)S(1)}) fusion(f32[512,4096]{1,0:T(8,128)} %get-tuple-element.26, f32[4096]{0:T(1024)S(1)} %get-tuple-element.11, f32[4096]{0:T(1024)S(1)} %get-tuple-element.12, f32[512,4096]{1,0:T(8,128)} %get-tuple-element.28), kind=kLoop, calls=%fused_computation.47 | loop fusion | flops 16775680 | bytes 16816128 | tf_op jit(solution)/shard_map/reduce_sum | solution.py:50
  159.1 9.7 %all-reduce.5 = (f32[512]{0:T(512)S(1)}, f32[512]{0:T(512)S(1)}) all-reduce(f32[512]{0:T(512)S(1)} %get-tuple-element.4, f32[512]{0:T(512)S(1)} %get-tuple-element.29), channel_id=1, replica_groups=mesh['batch'=8,'replica'=4,'proto'=4] {'proto'}, use_global_device_ids=true, to_apply=%region_8.0 | all-reduce | flops 1024 | bytes 8192 | tf_op jit(solution)/shard_map/psum | solution.py:25
  168.9 4.7 fusion.22
  173.6 4.7 fusion.21
  178.2 126.6 %all-reduce.1 = (f32[4096]{0:T(1024)S(1)}, f32[4096]{0:T(1024)S(1)}) all-reduce(f32[4096]{0:T(1024)S(1)} %fusion.21, f32[4096]{0:T(1024)S(1)} %fusion.22), channel_id=1, replica_groups=mesh['batch'=8,'replica'=4,'proto'=4] {'batch','replica'}, use_global_device_ids=true, to_apply=%region_10.0 | all-reduce | flops 8192 | bytes 65536 | tf_op jit(solution)/shard_map/psum | solution.py:24
  304.8 4.7 fusion.23
  309.5 4.7 fusion.24
  314.2 6.0 all-reduce.4
  320.2 5.0 fusion.26
  325.2 5.0 fusion.25
  330.1 125.5 %all-reduce = (f32[4096]{0:T(1024)S(1)}, f32[4096]{0:T(1024)S(1)}) all-reduce(f32[4096]{0:T(1024)S(1)} %fusion.25, f32[4096]{0:T(1024)S(1)} %fusion.26), channel_id=1, replica_groups=mesh['batch'=8,'replica'=4,'proto'=4] {'batch','replica'}, use_global_device_ids=true, to_apply=%region_14.0 | all-reduce | flops 8192 | bytes 65536 | tf_op jit(solution)/shard_map/psum | solution.py:24
  455.7 6.4 fusion.27
  462.1 5.3 fusion.28
  467.4 7.8 %all-reduce.3 = (f32[512]{0:T(512)S(1)}, f32[512]{0:T(512)S(1)}, f32[512]{0:T(512)S(1)}, f32[512]{0:T(512)S(1)}) all-reduce(f32[512]{0:T(512)S(1)} %fusion.28, f32[512]{0:T(512)S(1)} %get-tuple-element.6, f32[512]{0:T(512)S(1)} %get-tuple-element.5, ...), channel_id=1, replica_groups=mesh['batch'=8,'replica'=4,'proto'=4] {'proto'}, use_global_device_ids=true, to_apply=%region_16.0 | all-reduce | flops 2048 | bytes 16384 | tf_op jit(solution)/shard_map/psum | solution.py:25
  475.3 7.4 fusion.19
  482.7 2.6 scatter_custom_fusion
  485.3 12.2 %gather_fusion.1 = f32[512,4096]{1,0:T(8,128)} fusion(f32[512,4096]{1,0:T(8,128)} %fusion.19, s32[1024]{0:T(1024)S(1)} %pad_clamp_fusion), kind=kCustom, calls=%fused_computation.1 | custom fusion | bytes 16779264 | tf_op jit(solution)/shard_map/gather | solution.py:60
  497.5 11.4 %multiply_convert_fusion = (bf16[512,4096]{1,0:T(8,128)(2,1)}, f32[512,4096]{1,0:T(8,128)}) fusion(f32[512,4096]{1,0:T(8,128)} %gather_fusion.1, f32[512,4096]{1,0:T(8,128)} %get-tuple-element.26, f32[512]{0:T(512)S(1)} %get-tuple-element.16, f32[512]{0:T(512)S(1)} %get-tuple-element.13, f32[4096]{0:T(1024)S(1)} %get-tuple-element.7, ...), kind=kLoop, calls=%fused_computation.30 | loop fusion | flops 25165824 | bytes 29417472 | tf_op jit(solution)/shard_map/convert_element_type | solution.py:65
  509.0 12.2 %gather_fusion = f32[512,4096]{1,0:T(8,128)} fusion(f32[512,4096]{1,0:T(8,128)} %get-tuple-element.24, s32[1024]{0:T(1024)S(1)} %pad_clamp_fusion.1), kind=kCustom, calls=%fused_computation | custom fusion | bytes 16779264 | tf_op jit(solution)/shard_map/gather | solution.py:59
  521.2 7.3 multiply_convert_fusion.1
  530.5 3.4 fusion.58
  533.9 3.4 fusion.56
  537.4 4.9 fusion.47
  542.3 6.1 convolution_add_fusion
  548.4 48.4 %all-reduce.12.cloned.1.call-done = (f32[512,512]{1,0:T(8,128)}, f32[512,512]{1,0:T(8,128)}) async-done(((f32[512,512]{1,0:T(8,128)}, f32[512,512]{1,0:T(8,128)}), (f32[512,512]{1,0:T(8,128)}, f32[512,512]{1,0:T(8,128)})) %all-reduce.12.cloned.1.call-update) | async-done | bytes 2097168 | tf_op jit(solution)/shard_map/psum | solution.py:70
  604.7 116.6 %all-reduce.10.cloned.1.call-done = f32[4096,512]{1,0:T(8,128)} async-done(((f32[4096,512]{1,0:T(8,128)}), f32[4096,512]{1,0:T(8,128)}) %all-reduce.10.cloned.1.call-update) | async-done | bytes 8388624 | tf_op jit(solution)/shard_map/psum | solution.py:78
  721.3 6.1 fusion.15
  729.6 4.6 fusion.17
  (38 shorter events, 14.7 us)
Async XLA Ops:
  7.2 589.7 %all-reduce.12.cloned.1.call-start = ((), (), s32[]{:S(2)}) async-start(), calls=%async_computation.1 | async-start | bytes 4194304 | tf_op jit(solution)/shard_map/psum | solution.py:70
  12.8 8.5 %copy-start = (bf16[4096,512]{1,0:T(8,128)(2,1)S(1)}, bf16[4096,512]{1,0:T(8,128)(2,1)}, u32[]{:S(2)}) copy-start(bf16[4096,512]{1,0:T(8,128)(2,1)} %param.6) | copy-start | bytes 12582916
  12.8 8.5 %copy-start.7 = (bf16[512,512]{1,0:T(8,128)(2,1)S(1)}, bf16[512,512]{1,0:T(8,128)(2,1)}, u32[]{:S(2)}) copy-start(bf16[512,512]{1,0:T(8,128)(2,1)} %param.4) | copy-start | bytes 1572868
  475.3 7.4 copy-start.9
  521.2 9.3 %copy-start.1 = (bf16[4096,512]{1,0:T(8,128)(2,1)S(1)}, bf16[4096,512]{1,0:T(8,128)(2,1)}, u32[]{:S(2)}) copy-start(bf16[4096,512]{1,0:T(8,128)(2,1)} %param.6) | copy-start | bytes 12582916
  528.5 2.0 copy-start.6
  530.5 3.4 copy-start.4
  537.3 4.9 copy-start.8
  537.4 183.9 %all-reduce.10.cloned.1.call-start = ((), (), s32[]{:S(2)}) async-start(), calls=%async_computation | async-start | bytes 16777216 | tf_op jit(solution)/shard_map/psum | solution.py:78
  537.4 4.9 copy-start.5
  721.3 6.2 copy-start.2
  721.3 8.3 %copy-start.3 = (f32[4096,512]{1,0:T(8,128)S(1)}, f32[4096,512]{1,0:T(8,128)}, u32[]{:S(2)}) copy-start(f32[4096,512]{1,0:T(8,128)} %all-reduce.10.cloned.1.call-done) | copy-start | bytes 25165828
Sparse Core Ops, SparseCore 0:
  537.5 59.2 all-reduce.11
  601.1 120.0 all-reduce.9
where the time goes:
time: 749 us; the launch traced here: 741 us
  blocking collectives  401 us (54%)
  waiting for transfers between devices  165 us (22%)
  other arithmetic  98.8 us (13%)
  local copies, waits for them, and re-layouts  31.2 us (4%)
  matrix products  31.2 us (4%)
  between operations  14.5 us (2%)
    psum x3, blocking collectives, balance_single(): lax.psum(jnp.sum(codes, 0, keepdims=True), ('batch', 'replica'))  377 us
    psum x1, waiting for transfers between devices, per_device(): dunit_proto = lax.psum(local_grad, ('batch', 'replica'))  117 us
    psum x1, waiting for transfers between devices, per_device(): dunit_one, dunit_two = lax.psum((part_one, part_two), 'proto')  48.4 us
    psum x3, blocking collectives, balance_single(): codes = codes / lax.psum(jnp.sum(codes, 1, keepdims=True), 'proto')  23.6 us
    reduce_sum x4, other arithmetic, balance_single(): codes = codes / lax.psum(jnp.sum(codes, 1, keepdims=True), 'proto')  21.2 us
    reduce_sum x4, other arithmetic, balance_single(): jnp.sum(codes, 0, keepdims=True)  19.2 us
  transfers between devices with their start and end apart: 2, of which 2 were waited for; matrix products, arithmetic and copies ran while one was open for 3% of the time, Pallas kernels for 0%

commit v1 on v0

--- a/solution.py
+++ b/solution.py
@@ -21,7 +21,9 @@
 def balance_single(similarity_logits):
     codes = jnp.exp(similarity_logits / sink_eps)
     for step in range(ITERS):
-        codes = codes / lax.psum(jnp.sum(codes, 0, keepdims=True), ("batch", "replica"))
+        codes = codes / jnp.sum(
+            lax.all_gather(jnp.sum(codes, 0, keepdims=True), ("batch", "replica")), axis=0
+        )
         codes = codes / lax.psum(jnp.sum(codes, 1, keepdims=True), "proto")
     return codes
 

time: 749 us -> 644 us (0.86)
  blocking collectives: 401 us -> 296 us
    psum x3 -> x0, blocking collectives: 377 us -> none  [balance_single(): lax.psum(jnp.sum(codes, 0, keepdims=True), ('batch', 'replica'))]
    all_gather x0 -> x6, blocking collectives: none -> 272 us  [balance_single(): lax.all_gather(jnp.sum(codes, 0, keepdims=True), ('batch', 'replica'))]
where the time goes in v1:
time: 644 us; the launch traced here: 636 us
  blocking collectives  296 us (46%)
  waiting for transfers between devices  164 us (25%)
  other arithmetic  99.1 us (15%)
  local copies, waits for them, and re-layouts  31.7 us (5%)
  matrix products  31 us (5%)
  between operations  14.7 us (2%)
    all_gather x6, blocking collectives, balance_single(): lax.all_gather(jnp.sum(codes, 0, keepdims=True), ('batch', 'replica'))  272 us
    psum x1, waiting for transfers between devices, per_device(): dunit_proto = lax.psum(local_grad, ('batch', 'replica'))  117 us
    psum x1, waiting for transfers between devices, per_device(): dunit_one, dunit_two = lax.psum((part_one, part_two), 'proto')  47.1 us
    psum x3, blocking collectives, balance_single(): codes = codes / lax.psum(jnp.sum(codes, 1, keepdims=True), 'proto')  23.6 us
    reduce_sum x4, other arithmetic, balance_single(): codes = codes / lax.psum(jnp.sum(codes, 1, keepdims=True), 'proto')  21.2 us
    reduce_sum x4, other arithmetic, balance_single(): jnp.sum(codes, 0, keepdims=True)  19.2 us
  transfers between devices with their start and end apart: 2, of which 2 were waited for; matrix products, arithmetic and copies ran while one was open for 3% of the time, Pallas kernels for 0%

profile of v1, /device:TPU:1, one launch (start us, length us, event | category | flops | bytes accessed | tf_op | source)
XLA Modules:
  0.0 636.0 jit_solution(9008932449951717306)
XLA Ops:
  12.8 8.3 %fusion.32 = (f32[4096]{0:T(1024)S(1)}, f32[512,4096]{1,0:T(8,128)}) fusion(bf16[4096,512]{1,0:T(8,128)(2,1)} %param.6, f32[4096]{0:T(1024)S(1)} %add_rsqrt_fusion, bf16[512,512]{1,0:T(8,128)(2,1)} %param.4, f32[512]{0:T(512)S(1)} %add_rsqrt_fusion.2), kind=kOutput, calls=%fused_computation.50 | convolution fusion | flops 2158751744 | bytes 13142016 | tf_op jit(solution)/shard_map/dot_general | solution.py:39
  21.1 4.9 fusion.31
  26.0 44.3 %all-gather = f32[131072]{0:T(1024)S(1)} all-gather(f32[4096]{0:T(1024)S(1)} %get-tuple-element.19), channel_id=2, replica_groups=mesh['batch'=8,'replica'=4,'proto'=4] {'batch','replica'}, dimensions={0}, use_global_device_ids=true | all-gather | bytes 540672 | tf_op jit(solution)/shard_map/all_gather | solution.py:25
  70.5 42.0 %all-gather.3 = f32[131072]{0:T(1024)S(1)} all-gather(f32[4096]{0:T(1024)S(1)} %get-tuple-element.21), channel_id=5, replica_groups=mesh['batch'=8,'replica'=4,'proto'=4] {'batch','replica'}, dimensions={0}, use_global_device_ids=true | all-gather | bytes 540672 | tf_op jit(solution)/shard_map/all_gather | solution.py:25
  112.7 8.0 %fusion.30 = (f32[512]{0:T(512)S(1)}, f32[512]{0:T(512)S(1)}, f32[512]{0:T(512)S(1)}) fusion(f32[512,4096]{1,0:T(8,128)} %get-tuple-element.20, f32[4096]{0:T(1024)S(1)} %reduce.6, f32[4096]{0:T(1024)S(1)} %reduce.9, f32[512,4096]{1,0:T(8,128)} %get-tuple-element.22), kind=kLoop, calls=%fused_computation.47 | loop fusion | flops 16775680 | bytes 16816128 | tf_op jit(solution)/shard_map/reduce_sum | solution.py:52
  120.7 9.7 %all-reduce.2 = (f32[512]{0:T(512)S(1)}, f32[512]{0:T(512)S(1)}) all-reduce(f32[512]{0:T(512)S(1)} %get-tuple-element.4, f32[512]{0:T(512)S(1)} %get-tuple-element.23), channel_id=1, replica_groups=mesh['batch'=8,'replica'=4,'proto'=4] {'proto'}, use_global_device_ids=true, to_apply=%region_8.0 | all-reduce | flops 1024 | bytes 8192 | tf_op jit(solution)/shard_map/psum | solution.py:27
  130.5 4.7 fusion.22
  135.1 45.6 %all-gather.4 = f32[131072]{0:T(1024)S(1)} all-gather(f32[4096]{0:T(1024)S(1)} %fusion.22), channel_id=6, replica_groups=mesh['batch'=8,'replica'=4,'proto'=4] {'batch','replica'}, dimensions={0}, use_global_device_ids=true | all-gather | bytes 540672 | tf_op jit(solution)/shard_map/all_gather | solution.py:25
  180.9 4.7 fusion.23
  185.6 4.7 fusion.21
  190.3 42.0 %all-gather.1 = f32[131072]{0:T(1024)S(1)} all-gather(f32[4096]{0:T(1024)S(1)} %fusion.21), channel_id=3, replica_groups=mesh['batch'=8,'replica'=4,'proto'=4] {'batch','replica'}, dimensions={0}, use_global_device_ids=true | all-gather | bytes 540672 | tf_op jit(solution)/shard_map/all_gather | solution.py:25
  232.5 4.7 fusion.24
  237.2 6.0 all-reduce.1
  243.2 5.0 fusion.26
  248.1 45.1 %all-gather.5 = f32[131072]{0:T(1024)S(1)} all-gather(f32[4096]{0:T(1024)S(1)} %fusion.26), channel_id=7, replica_groups=mesh['batch'=8,'replica'=4,'proto'=4] {'batch','replica'}, dimensions={0}, use_global_device_ids=true | all-gather | bytes 540672 | tf_op jit(solution)/shard_map/all_gather | solution.py:25
  293.4 6.4 %fusion.27 = (f32[512]{0:T(512)S(1)}, f32[512]{0:T(512)S(1)}) fusion(f32[4096]{0:T(1024)S(1)} %reduce.11, f32[512]{0:T(512)S(1)} %get-tuple-element.12, f32[4096]{0:T(1024)S(1)} %reduce.10, f32[512]{0:T(512)S(1)} %get-tuple-element.14, f32[4096]{0:T(1024)S(1)} %reduce.9, f32[512,4096]{1,0:T(8,128)} %get-tuple-element.22), kind=kLoop, calls=%fused_computation.44 | loop fusion | flops 18873344 | bytes 8445952 | tf_op jit(solution)/shard_map/reduce_sum | solution.py:27
  299.8 5.0 fusion.25
  304.8 53.2 %all-gather.2 = f32[131072]{0:T(1024)S(1)} all-gather(f32[4096]{0:T(1024)S(1)} %fusion.25), channel_id=4, replica_groups=mesh['batch'=8,'replica'=4,'proto'=4] {'batch','replica'}, dimensions={0}, use_global_device_ids=true | all-gather | bytes 540672 | tf_op jit(solution)/shard_map/all_gather | solution.py:25
  358.2 5.3 fusion.28
  363.5 7.8 %all-reduce = (f32[512]{0:T(512)S(1)}, f32[512]{0:T(512)S(1)}, f32[512]{0:T(512)S(1)}, f32[512]{0:T(512)S(1)}) all-reduce(f32[512]{0:T(512)S(1)} %fusion.28, f32[512]{0:T(512)S(1)} %get-tuple-element.6, f32[512]{0:T(512)S(1)} %get-tuple-element.5, f32[512]{0:T(512)S(1)} %get-tuple-element.3), channel_id=1, replica_groups=mesh['batch'=8,'replica'=4,'proto'=4] {'proto'}, use_global_device_ids=true, to_apply=%region_16.0 | all-reduce | flops 2048 | bytes 16384 | tf_op jit(solution)/shard_map/psum | solution.py:27
  371.3 7.4 %fusion.19 = f32[512,4096]{1,0:T(8,128)} fusion(f32[512]{0:T(512)S(1)} %get-tuple-element.9, f32[4096]{0:T(1024)S(1)} %reduce.11, f32[512]{0:T(512)S(1)} %get-tuple-element.12, f32[4096]{0:T(1024)S(1)} %reduce.10, f32[512]{0:T(512)S(1)} %get-tuple-element.14, f32[4096]{0:T(1024)S(1)} %reduce.9, f32[512,4096]{1,0:T(8,128)} %get-tuple-element.22), kind=kLoop, calls=%fused_computation.28 | loop fusion | flops 14680064 | bytes 16832512 | tf_op jit(solution)/shard_map/div | solution.py:27
  381.2 12.2 %gather_fusion.1 = f32[512,4096]{1,0:T(8,128)} fusion(f32[512,4096]{1,0:T(8,128)} %fusion.19, s32[1024]{0:T(1024)S(1)} %pad_clamp_fusion), kind=kCustom, calls=%fused_computation.1 | custom fusion | bytes 16779264 | tf_op jit(solution)/shard_map/gather | solution.py:62
  393.4 11.4 %multiply_convert_fusion = (bf16[512,4096]{1,0:T(8,128)(2,1)}, f32[512,4096]{1,0:T(8,128)}) fusion(f32[512,4096]{1,0:T(8,128)} %gather_fusion.1, f32[512,4096]{1,0:T(8,128)} %get-tuple-element.20, f32[512]{0:T(512)S(1)} %get-tuple-element.10, f32[512]{0:T(512)S(1)} %get-tuple-element.7, f32[4096]{0:T(1024)S(1)} %reduce.8, f32[512]{0:T(512)S(1)} %get-tuple-element.11, ...), kind=kLoop, calls=%fused_computation.30 | loop fusion | flops 25165824 | bytes 29417472 | tf_op jit(solution)/shard_map/convert_element_type | solution.py:67
  404.8 12.2 %gather_fusion = f32[512,4096]{1,0:T(8,128)} fusion(f32[512,4096]{1,0:T(8,128)} %get-tuple-element.18, s32[1024]{0:T(1024)S(1)} %pad_clamp_fusion.1), kind=kCustom, calls=%fused_computation | custom fusion | bytes 16779264 | tf_op jit(solution)/shard_map/gather | solution.py:61
  417.0 7.3 %multiply_convert_fusion.1 = bf16[512,4096]{1,0:T(8,128)(2,1)S(1)} fusion(f32[512,4096]{1,0:T(8,128)} %gather_fusion, f32[512,4096]{1,0:T(8,128)} %get-tuple-element.22, f32[512]{0:T(512)S(1)} %get-tuple-element.8), kind=kLoop, calls=%fused_computation.33 | loop fusion | flops 10485760 | bytes 20973568 | tf_op jit(solution)/shard_map/convert_element_type | solution.py:64
  429.8 3.4 fusion.56
  433.3 4.9 fusion.47
  438.2 6.1 convolution_add_fusion
  444.3 47.1 %all-reduce.9.cloned.1.call-done = (f32[512,512]{1,0:T(8,128)}, f32[512,512]{1,0:T(8,128)}) async-done(((f32[512,512]{1,0:T(8,128)}, f32[512,512]{1,0:T(8,128)}), (f32[512,512]{1,0:T(8,128)}, f32[512,512]{1,0:T(8,128)})) %all-reduce.9.cloned.1.call-update) | async-done | bytes 2097168 | tf_op jit(solution)/shard_map/psum | solution.py:72
  499.3 116.6 %all-reduce.7.cloned.1.call-done = f32[4096,512]{1,0:T(8,128)} async-done(((f32[4096,512]{1,0:T(8,128)}), f32[4096,512]{1,0:T(8,128)}) %all-reduce.7.cloned.1.call-update) | async-done | bytes 8388624 | tf_op jit(solution)/shard_map/psum | solution.py:80
  615.9 6.1 fusion.15
  624.2 4.6 fusion.17
  (53 shorter events, 24.5 us)
Async XLA Ops:
  7.2 484.2 %all-reduce.9.cloned.1.call-start = ((), (), s32[]{:S(2)}) async-start(), calls=%async_computation.1 | async-start | bytes 4194304 | tf_op jit(solution)/shard_map/psum | solution.py:72
  12.8 8.3 %copy-start = (bf16[4096,512]{1,0:T(8,128)(2,1)S(1)}, bf16[4096,512]{1,0:T(8,128)(2,1)}, u32[]{:S(2)}) copy-start(bf16[4096,512]{1,0:T(8,128)(2,1)} %param.6) | copy-start | bytes 12582916
  12.8 8.3 %copy-start.8 = (bf16[512,512]{1,0:T(8,128)(2,1)S(1)}, bf16[512,512]{1,0:T(8,128)(2,1)}, u32[]{:S(2)}) copy-start(bf16[512,512]{1,0:T(8,128)(2,1)} %param.5) | copy-start | bytes 1572868
  371.3 7.4 %copy-start.9 = (s32[1,512]{1,0:T(1,128)S(1)}, s32[1,512]{1,0:T(1,128)}, u32[]{:S(2)}) copy-start(s32[1,512]{1,0:T(1,128)} %param.7) | copy-start | bytes 6148
  417.0 9.3 %copy-start.1 = (bf16[4096,512]{1,0:T(8,128)(2,1)S(1)}, bf16[4096,512]{1,0:T(8,128)(2,1)}, u32[]{:S(2)}) copy-start(bf16[4096,512]{1,0:T(8,128)(2,1)} %param.6) | copy-start | bytes 12582916
  424.3 2.0 copy-start.6
  426.4 3.4 copy-start.4
  429.8 3.5 copy-start.7
  433.2 182.6 %all-reduce.7.cloned.1.call-start = ((), (), s32[]{:S(2)}) async-start(), calls=%async_computation | async-start | bytes 16777216 | tf_op jit(solution)/shard_map/psum | solution.py:80
  433.3 4.9 copy-start.5
  615.8 6.1 copy-start.2
  615.8 8.3 %copy-start.3 = (f32[4096,512]{1,0:T(8,128)S(1)}, f32[4096,512]{1,0:T(8,128)}, u32[]{:S(2)}) copy-start(f32[4096,512]{1,0:T(8,128)} %all-reduce.7.cloned.1.call-done) | copy-start | bytes 25165828
Sparse Core Ops, SparseCore 0:
  433.4 57.9 all-reduce.8
  495.7 120.0 all-reduce.6
